TPU v7x, 32 devices: a whole 2x2x4 slice. The times are simulated.
32 devices in a mesh: group: 2 (over x), cand: 16 (over z, y, core).
Axes of the slice: x: 2, y: 2, z: 4, core: 2. Of those that a mesh axis runs over, the one named last changes fastest.
Arguments:
- embeddings: bfloat16 [64, 1024, 768], P(('group', 'cand')), parts along dimension 0
- lengths: int32 [64], P(('group', 'cand')), parts along dimension 0, may hold values from 256 to 1024, as said below
Outputs:
- consensus: float32 [64, 1024], P(('group', 'cand')), parts along dimension 0
There are 2 independent parts, one for each index of `group`. A program takes and returns all parts, laid end to end along the dimension named above; each array names one. Nothing has to cross between parts.
Inputs may be any that keep to these rules, and one draw needn't show every extreme that they name: `lengths`: at least one answer of every prompt has exactly 1024 tokens; every answer has 256 tokens or more.
All inputs are finite; a program needn't handle non-finite values.
Results may differ from a plain program's by a relative error of at most 0.0005.
Values may be sent and summed in bfloat16 or wider, within the bound.
A program may use at most 64 MiB of HBM per device.

v0:
```python
import jax
import jax.numpy as jnp
from jax import lax
from jax.sharding import PartitionSpec as P

INV_TEMP = 256.0


def from_behind(shard, axis, by):
    count = lax.axis_size(axis)
    return lax.ppermute(shard, axis, [(i, (i + by) % count) for i in range(count)])


def unit_rows(embeddings):
    values = embeddings.astype(jnp.float32)
    scale = lax.rsqrt(jnp.sum(values * values, axis=-1, keepdims=True) + 1e-06)
    return (values * scale).astype(jnp.bfloat16)


def soft_terms(left, left_valid, right, right_valid):
    scores = jnp.einsum("te,bse->bts", left, right, preferred_element_type=jnp.float32) * INV_TEMP
    row_scores = jnp.where(right_valid[:, None, :] > 0.5, scores, -1e30)
    row_peak = jnp.max(row_scores, axis=2, keepdims=True)
    row_terms = (
        row_peak[..., 0] + jnp.log(jnp.sum(jnp.exp(row_scores - row_peak), axis=2))
    ) / INV_TEMP
    col_scores = jnp.where(left_valid[None, :, None] > 0.5, scores, -1e30)
    col_peak = jnp.max(col_scores, axis=1, keepdims=True)
    col_terms = (
        col_peak[:, 0, :] + jnp.log(jnp.sum(jnp.exp(col_scores - col_peak), axis=1))
    ) / INV_TEMP
    return (row_terms, col_terms)


def cross_block(unit, valid, partner):
    their_unit, their_mask = partner
    their_valid = their_mask.astype(jnp.float32)
    row_list = []
    col_total = jnp.zeros(their_valid.shape, jnp.float32)
    for slot in range(unit.shape[0]):
        row_terms, col_terms = soft_terms(unit[slot], valid[slot], their_unit, their_valid)
        row_list.append(jnp.sum(row_terms, axis=0))
        col_total = col_total + col_terms
    return (jnp.stack(row_list), col_total)


def shards(embeddings, lengths):
    answers = embeddings.shape[0]
    length = embeddings.shape[1]
    unit = unit_rows(embeddings)
    valid = (lax.broadcasted_iota(jnp.int32, (answers, length), 1) < lengths[:, None]).astype(
        jnp.float32
    )
    own_block = (unit, valid.astype(jnp.bfloat16))
    totals = jnp.zeros((answers, length), jnp.float32)
    first = from_behind((own_block[0], own_block[1]), "cand", 1)
    second = from_behind((own_block[0], own_block[1]), "cand", 2)
    row_terms, col_terms = soft_terms(unit[0], valid[0], unit[1:], valid[1:])
    totals = totals.at[0].add(jnp.sum(row_terms, axis=0))
    totals = totals.at[1:].add(col_terms)
    rows_first, cols_first = cross_block(unit, valid, first)
    returned_first = from_behind(cols_first, "cand", -1)
    rows_second, cols_second = cross_block(unit, valid, second)
    returned_second = from_behind(cols_second, "cand", -2)
    totals = totals + rows_first + rows_second + returned_first + returned_second
    return totals * valid / (answers - 1 + 4 * answers)


def solution(mesh):
    return jax.shard_map(
        shards,
        mesh=mesh,
        in_specs=(P(("group", "cand"), None, None), P(("group", "cand"))),
        out_specs=P(("group", "cand"), None),
        check_vma=False,
    )
```

profile of v0, /device:TPU:1, one launch (start us, length us, event | category | flops | bytes accessed | tf_op | source)
XLA Modules:
  0.0 145.2 jit_solution(10423566783832293790)
XLA Ops:
  0.0 2.6 %fusion.16 = f32[2,1024]{1,0:T(2,128)S(1)} fusion(bf16[2,1024,768]{2,1,0:T(8,128)(2,1)} %param.6), kind=kLoop, calls=%fused_computation.34 | loop fusion | flops 4716544 | bytes 3153920 | tf_op jit(solution)/shard_map/reduce_sum | solution.py:16
  2.6 2.5 %fusion.17 = bf16[2,1024,768]{2,1,0:T(8,128)(2,1)S(1)} fusion(bf16[2,1024,768]{2,1,0:T(8,128)(2,1)} %param.6, f32[2,1024]{1,0:T(2,128)S(1)} %add_rsqrt_fusion), kind=kLoop, calls=%fused_computation.35 | loop fusion | flops 4718592 | bytes 6299648 | tf_op jit(solution)/shard_map/convert_element_type | solution.py:17
  5.1 2.7 %collective-permute-start.1 = (bf16[2,1024,768]{2,1,0:T(8,128)(2,1)S(1)}, bf16[2,1024,768]{2,1,0:T(8,128)(2,1)S(1)}, u32[]{:S(2)}, u32[]{:S(2)}) collective-permute-start(bf16[2,1024,768]{2,1,0:T(8,128)(2,1)S(1)} %fusion.17), channel_id=1, source_target_pairs={{0,1},{1,2},{2,3},{3,4},{4,5},{5,6},{6,7},{7,8},{8,9},{9,10},{10,1... | collective-permute-start | bytes 9437192 | tf_op jit(solution)/shard_map/ppermute | solution.py:11
  7.8 0.1 fusion.41
  7.8 1.2 collective-permute-start.2
  9.1 0.3 collective-permute-start
  9.4 1.2 collective-permute-start.3
  10.7 1.8 %fusion.18 = (f32[1024]{0:T(1024)S(1)}, f32[1024,1024]{1,0:T(8,128)S(1)}) fusion(pred[1024]{0:T(1024)(128)(4,1)S(1)} %get-tuple-element.40, bf16[2,1024,768]{2,1,0:T(8,128)(2,1)S(1)} %fusion.17), kind=kOutput, calls=%fused_computation.40 | convolution fusion | flops 1613757440 | bytes 7345152 | tf_op jit(solution)/shard_map/te,bse->bts/dot_general | solution.py:21
  12.5 1.9 %exponential_reduce_fusion.1 = (f32[1024]{0:T(1024)S(1)}, f32[1024]{0:T(1024)S(1)}) fusion(f32[1024,1024]{1,0:T(8,128)S(1)} %get-tuple-element.54, f32[1024]{0:T(1024)S(1)} %get-tuple-element.53, pred[1024]{0:T(1024)(128)(4,1)S(1)} %get-tuple-element.40, pred[1024]{0:T(1024)(128)(4,1)S(1)} %get-tuple-element.39), kind=kLoop, calls=%fused_computation.39 | loop fusion | flops 6289408 | bytes 4208640 | tf_op jit(solution)/shard_map/reduce_sum | solution.py:25
  14.5 1.0 exponential_reduce_fusion
  15.5 59.6 %collective-permute-done.2 = bf16[2,1024]{1,0:T(2,128)(2,1)S(1)} collective-permute-done((bf16[2,1024]{1,0:T(2,128)(2,1)S(1)}, bf16[2,1024]{1,0:T(2,128)(2,1)S(1)}, u32[]{:S(2)}, u32[]{:S(2)}) %collective-permute-start.2) | collective-permute-done | bytes 4128 | tf_op jit(solution)/shard_map/ppermute | solution.py:11
  75.2 3.7 %bitcast_reduce_fusion.7 = (f32[2,1024]{1,0:T(2,128)S(1)}, f32[2,1024,1024]{2,1,0:T(8,128)S(1)}) fusion(pred[2,1024]{1,0:T(4,128)(4,1)S(1)} %convert_compare_fusion.1, bf16[2,1024,768]{2,1,0:T(8,128)(2,1)S(1)} %collective-permute-done.1, bf16[2,1024,768]{2,1,0:T(8,128)(2,1)S(1)} %fusion.17), kind=kOutput, calls=%fused_computation.29 | convolution fusion | flops 3227514880 | bytes 13119488 | tf_op jit(solution)/shard_map/te,bse->bts/dot_general | solution.py:21
  78.8 6.1 %fusion.15 = (f32[2,1024]{1,0:T(2,128)S(1)}, f32[2,1024]{1,0:T(2,128)S(1)}, f32[2,1024]{1,0:T(2,128)S(1)}, f32[2,1024,1024]{2,1,0:T(8,128)S(1)}) fusion(f32[2,1024,1024]{2,1,0:T(8,128)S(1)} %get-tuple-element.50, f32[2,1024]{1,0:T(2,128)S(1)} %get-tuple-element.49, pred[2,1024]{1,0:T(4,128)(4,1)S(1)} %convert_compare_fusion.1, ...), kind=kOutput, calls=%fused_computation.31 | convolution fusion | flops 3240093696 | bytes 21533696 | tf_op jit(solution)/shard_map/te,bse->bts/dot_general | solution.py:21
  85.0 3.2 %fusion.13 = (f32[2,1024]{1,0:T(2,128)S(1)}, f32[2,1024]{1,0:T(2,128)S(1)}) fusion(f32[2,1024,1024]{2,1,0:T(8,128)S(1)} %get-tuple-element.51, f32[2,1024]{1,0:T(2,128)S(1)} %get-tuple-element.41, pred[2,1024]{1,0:T(4,128)(4,1)S(1)} %convert_compare_fusion.1, pred[1024]{0:T(1024)(128)(4,1)S(1)} %get-tuple-element.40), kind=kLoop, calls=%fused_computation.27 | loop fusion | flops 12578816 | bytes 8416256 | tf_op jit(solution)/shard_map/reduce_sum | solution.py:25
  88.1 24.3 %collective-permute-done.3 = bf16[2,1024,768]{2,1,0:T(8,128)(2,1)S(1)} collective-permute-done((bf16[2,1024,768]{2,1,0:T(8,128)(2,1)S(1)}, bf16[2,1024,768]{2,1,0:T(8,128)(2,1)S(1)}, u32[]{:S(2)}, u32[]{:S(2)}) %collective-permute-start.3) | collective-permute-done | bytes 3145760 | tf_op jit(solution)/shard_map/ppermute | solution.py:11
  112.4 5.7 %bitcast_reduce_fusion.5 = (f32[2,1024]{1,0:T(2,128)S(1)}, f32[2,1024,1024]{2,1,0:T(8,128)}) fusion(pred[2,1024]{1,0:T(4,128)(4,1)S(1)} %convert_compare_fusion, bf16[2,1024,768]{2,1,0:T(8,128)(2,1)S(1)} %collective-permute-done.3, bf16[2,1024,768]{2,1,0:T(8,128)(2,1)S(1)} %fusion.17), kind=kOutput, calls=%fused_computation.21 | convolution fusion | flops 3227514880 | bytes 13119488 | tf_op jit(solution)/shard_map/te,bse->bts/dot_general | solution.py:21
  118.1 10.8 %fusion.11 = (f32[2,1024]{1,0:T(2,128)S(1)}, f32[2,1024]{1,0:T(2,128)S(1)}, f32[2,1024]{1,0:T(2,128)S(1)}, f32[2,1024]{1,0:T(2,128)S(1)}, f32[2,1024,1024]{2,1,0:T(8,128)S(1)}) fusion(f32[2,1024,1024]{2,1,0:T(8,128)} %get-tuple-element.48, f32[2,1024]{1,0:T(2,128)S(1)} %get-tuple-element.47, pred[2,1024]{1,0:T(4,128)(4,1)S(1)} %convert_compare_fusion, ...), kind=kOutput, calls=%fused_computation.23 | convolution fusion | flops 3248480256 | bytes 29938688 | tf_op jit(solution)/shard_map/te,bse->bts/dot_general | solution.py:21
  128.9 8.4 %fusion.9 = (f32[2,1024]{1,0:T(2,128)S(1)}, f32[2,1024]{1,0:T(2,128)S(1)}, f32[2,1024]{1,0:T(2,128)S(1)}, f32[2,1024]{1,0:T(2,128)S(1)}) fusion(f32[2,1024,1024]{2,1,0:T(8,128)S(1)} %get-tuple-element.52, f32[2,1024]{1,0:T(2,128)S(1)} %get-tuple-element.42, pred[2,1024]{1,0:T(4,128)(4,1)S(1)} %convert_compare_fusion, ...), kind=kLoop, calls=%fused_computation.19 | loop fusion | flops 29351936 | bytes 25227264 | tf_op jit(solution)/shard_map/reduce_sum | solution.py:25
  137.3 2.0 %fusion.1 = f32[2,1024]{1,0:T(2,128)S(1)} fusion(f32[2,1024,1024]{2,1,0:T(8,128)S(1)} %get-tuple-element.52, f32[2,1024]{1,0:T(2,128)S(1)} %get-tuple-element.36, pred[1024]{0:T(1024)(128)(4,1)S(1)} %get-tuple-element.40), kind=kLoop, calls=%fused_computation.3 | loop fusion | flops 8386560 | bytes 8406016 | tf_op jit(solution)/shard_map/reduce_sum | solution.py:30
  139.3 2.1 %collective-permute-start.5 = (f32[2,1024]{1,0:T(2,128)S(1)}, f32[2,1024]{1,0:T(2,128)S(1)}, u32[]{:S(2)}, u32[]{:S(2)}) collective-permute-start(f32[2,1024]{1,0:T(2,128)S(1)} %add_multiply_fusion), channel_id=1, source_target_pairs={{0,14},{1,15},{2,0},{3,1},{4,2},{5,3},{6,4},{7,5},{8,6},{9,7},{10,... | collective-permute-start | bytes 24584 | tf_op jit(solution)/shard_map/ppermute | solution.py:11
  141.4 0.1 collective-permute-start.4
  141.6 0.6 collective-permute-done.5
  142.2 2.4 %collective-permute-done.4 = f32[2,1024]{1,0:T(2,128)S(1)} collective-permute-done((f32[2,1024]{1,0:T(2,128)S(1)}, f32[2,1024]{1,0:T(2,128)S(1)}, u32[]{:S(2)}, u32[]{:S(2)}) %collective-permute-start.4) | collective-permute-done | bytes 8224 | tf_op jit(solution)/shard_map/ppermute | solution.py:11
  144.5 0.7 fusion.42
  (18 shorter events, 0.2 us)
Async XLA Ops:
  0.0 7.8 %copy-start = (s32[2]{0:T(128)S(1)}, s32[2]{0:T(128)}, u32[]{:S(2)}) copy-start(s32[2]{0:T(128)} %param.7) | copy-start | bytes 28
  5.1 70.1 %collective-permute-start.1 = (bf16[2,1024,768]{2,1,0:T(8,128)(2,1)S(1)}, bf16[2,1024,768]{2,1,0:T(8,128)(2,1)S(1)}, u32[]{:S(2)}, u32[]{:S(2)}) collective-permute-start(bf16[2,1024,768]{2,1,0:T(8,128)(2,1)S(1)} %fusion.17), channel_id=1, source_target_pairs={{0,1},{1,2},{2,3},{3,4},{4,5},{5,6},{6,7},{7,8},{8,9},{9,10},{10,1... | collective-permute-start | bytes 9437192 | tf_op jit(solution)/shard_map/ppermute | solution.py:11
  7.8 67.3 %collective-permute-start.2 = (bf16[2,1024]{1,0:T(2,128)(2,1)S(1)}, bf16[2,1024]{1,0:T(2,128)(2,1)S(1)}, u32[]{:S(2)}, u32[]{:S(2)}) collective-permute-start(bf16[2,1024]{1,0:T(2,128)(2,1)S(1)} %get-tuple-element.46), channel_id=1, source_target_pairs={{0,2},{1,3},{2,4},{3,5},{4,6},{5,7},{6,8},{7,9},{8,10},{9,11},{10,... | collective-permute-start | bytes 12296 | tf_op jit(solution)/shard_map/ppermute | solution.py:11
  9.1 66.0 %collective-permute-start = (bf16[2,1024]{1,0:T(2,128)(2,1)S(1)}, bf16[2,1024]{1,0:T(2,128)(2,1)S(1)}, u32[]{:S(2)}, u32[]{:S(2)}) collective-permute-start(bf16[2,1024]{1,0:T(2,128)(2,1)S(1)} %get-tuple-element.46), channel_id=1, source_target_pairs={{0,1},{1,2},{2,3},{3,4},{4,5},{5,6},{6,7},{7,8},{8,9},{9,10},{10,1... | collective-permute-start | bytes 12296 | tf_op jit(solution)/shard_map/ppermute | solution.py:11
  9.4 103.1 %collective-permute-start.3 = (bf16[2,1024,768]{2,1,0:T(8,128)(2,1)S(1)}, bf16[2,1024,768]{2,1,0:T(8,128)(2,1)S(1)}, u32[]{:S(2)}, u32[]{:S(2)}) collective-permute-start(bf16[2,1024,768]{2,1,0:T(8,128)(2,1)S(1)} %fusion.17), channel_id=1, source_target_pairs={{0,2},{1,3},{2,4},{3,5},{4,6},{5,7},{6,8},{7,9},{8,10},{9,11},{10,... | collective-permute-start | bytes 9437192 | tf_op jit(solution)/shard_map/ppermute | solution.py:11
  78.8 6.1 %copy-start.2 = (f32[2,1024,1024]{2,1,0:T(8,128)}, f32[2,1024,1024]{2,1,0:T(8,128)S(1)}, u32[]{:S(2)}) copy-start(f32[2,1024,1024]{2,1,0:T(8,128)S(1)} %get-tuple-element.50) | copy-start | bytes 25165828
  112.4 5.7 %copy-start.1 = (bf16[2,1024,768]{2,1,0:T(8,128)(2,1)}, bf16[2,1024,768]{2,1,0:T(8,128)(2,1)S(1)}, u32[]{:S(2)}) copy-start(bf16[2,1024,768]{2,1,0:T(8,128)(2,1)S(1)} %collective-permute-done.3) | copy-start | bytes 9437188
  139.3 2.9 %collective-permute-start.5 = (f32[2,1024]{1,0:T(2,128)S(1)}, f32[2,1024]{1,0:T(2,128)S(1)}, u32[]{:S(2)}, u32[]{:S(2)}) collective-permute-start(f32[2,1024]{1,0:T(2,128)S(1)} %add_multiply_fusion), channel_id=1, source_target_pairs={{0,14},{1,15},{2,0},{3,1},{4,2},{5,3},{6,4},{7,5},{8,6},{9,7},{10,... | collective-permute-start | bytes 24584 | tf_op jit(solution)/shard_map/ppermute | solution.py:11
  141.4 3.1 %collective-permute-start.4 = (f32[2,1024]{1,0:T(2,128)S(1)}, f32[2,1024]{1,0:T(2,128)S(1)}, u32[]{:S(2)}, u32[]{:S(2)}) collective-permute-start(f32[2,1024]{1,0:T(2,128)S(1)} %add_multiply_fusion.1), channel_id=1, source_target_pairs={{0,15},{1,0},{2,1},{3,2},{4,3},{5,4},{6,5},{7,6},{8,7},{9,8},{10,9... | collective-permute-start | bytes 24584 | tf_op jit(solution)/shard_map/ppermute | solution.py:11
where the time goes:
time: 145 us
  waiting for transfers between devices  86.9 us (60%)
  matrix products  28 us (19%)
  other arithmetic  22.6 us (16%)
  starting transfers between devices  7.58 us (5%)
    ppermute x6, waiting for transfers between devices, from_behind(): lax.ppermute(shard, axis, [(i, (i + by) % count) for i in range(count)])  86.9 us
    dot_general x5, matrix products, soft_terms(): jnp.einsum('te,bse->bts', left, right, preferred_element_type=jnp.float32)  28 us
    reduce_sum x3, other arithmetic, soft_terms(): jnp.sum(jnp.exp(row_scores - row_peak), axis=2)  13.5 us
    ppermute x6, starting transfers between devices, from_behind(): lax.ppermute(shard, axis, [(i, (i + by) % count) for i in range(count)])  7.58 us
    reduce_sum x2, other arithmetic, soft_terms(): jnp.sum(jnp.exp(col_scores - col_peak), axis=1)  3.01 us
  transfers between devices with their start and end apart: 6, of which 4 were waited for; matrix products, arithmetic and copies ran while one was open for 12% of the time, Pallas kernels for 0%

commit v1 on v0

v1 whole, which is shorter than its diff:
```python
import functools
import math

import jax
import jax.numpy as jnp
from jax import lax
from jax.experimental import pallas as pl
from jax.experimental.pallas import tpu as pltpu
from jax.sharding import PartitionSpec as P

MESH = pl.DeviceIdType.MESH
INV_TEMP = 256.0
LOW = -1e30
ROWS = 128


def unit_rows(raw):
    values = raw.astype(jnp.float32)
    scale = lax.rsqrt(jnp.sum(values * values, axis=-1, keepdims=True) + 1e-06)
    return (values * scale).astype(jnp.bfloat16)


def kernel(
    n, x_hbm, lens_ref, out_ref,
    raw, units, fresh, lens, bias, peak, mass, total, back,
    local_sem, send_sem, recv_sem,
):
    answers, length = x_hbm.shape[0], x_hbm.shape[1]
    chunks = length // ROWS
    me = lax.axis_index("cand")
    parity = lax.rem(me, 2)
    partner = me + 1 - 2 * parity
    other = lax.rem(me + n - 1 + 2 * parity, n)

    barrier = pltpu.get_barrier_semaphore()
    for device in (partner, other):
        pl.semaphore_signal(barrier, inc=1, device_id={"cand": device}, device_id_type=MESH)
    local = pltpu.make_async_copy(x_hbm, raw.at[0], local_sem)
    local.start()
    pl.semaphore_wait(barrier, 2)

    def remote(src, dst, sem, device):
        return pltpu.make_async_remote_copy(
            src_ref=src, dst_ref=dst, send_sem=send_sem.at[sem], recv_sem=recv_sem.at[sem],
            device_id={"cand": device}, device_id_type=MESH,
        )

    def piece(k):
        rows = pl.ds(pl.multiple_of(k * ROWS, ROWS), ROWS)
        return remote(x_hbm.at[:, rows], raw.at[2, :, rows], k, other)

    lens_c = remote(lens_ref, lens.at[1], chunks, partner)
    lens_r = remote(lens_ref, lens.at[2], chunks + 1, other)
    block_c = remote(x_hbm, raw.at[1], chunks + 2, partner)
    lens_r.start()
    lens_c.start()
    for k in range(chunks):
        piece(k).start()
        if k == 0:
            block_c.start()

    lane = lax.broadcasted_iota(jnp.int32, (1, length), 1)
    eye = lax.broadcasted_iota(jnp.int32, (ROWS, ROWS), 0) == lax.broadcasted_iota(
        jnp.int32, (ROWS, ROWS), 1
    )
    total[...] = jnp.zeros_like(total)
    peak[...] = jnp.full_like(peak, LOW)
    mass[...] = jnp.zeros_like(mass)

    def set_bias(slot, counts):
        for a in range(answers):
            bias[slot * answers + a] = jnp.where(lane < counts[a : a + 1, 0:1], 0.0, LOW)

    def normalise(slot):
        def one(i, carry):
            a, k = i // chunks, lax.rem(i, chunks)
            rows = pl.ds(pl.multiple_of(k * ROWS, ROWS), ROWS)
            units[slot * answers + a, rows] = unit_rows(raw[slot, a, rows])
            return carry

        lax.fori_loop(0, answers * chunks, one, 0)

    def tile(query, row_slot, k, left, pair):
        cols = pl.ds(pl.multiple_of(k * ROWS, ROWS), ROWS)
        row_bias = jnp.broadcast_to(bias[row_slot, :, cols], (ROWS, ROWS))
        row_bias = jnp.sum(jnp.where(eye, row_bias, 0.0), axis=1, keepdims=True)
        scores = lax.dot_general(
            query, units[left], (((1,), (1,)), ((), ())), preferred_element_type=jnp.float32
        )
        scores = scores * (INV_TEMP / math.log(2.0)) + bias[left] + row_bias
        top = jnp.max(scores, axis=1, keepdims=True)
        row_sum = jnp.sum(jnp.exp2(scores - top), axis=1, keepdims=True)
        term = (top + jnp.log2(row_sum)) * (math.log(2.0) / INV_TEMP)
        term = jnp.sum(jnp.where(eye, jnp.broadcast_to(term, (ROWS, ROWS)), 0.0), axis=0, keepdims=True)
        total[row_slot, :, cols] = total[row_slot, :, cols] + term
        before = peak[pair]
        now = jnp.maximum(before, jnp.max(scores, axis=0, keepdims=True))
        peak[pair] = now
        mass[pair] = mass[pair] * jnp.exp2(before - now) + jnp.sum(
            jnp.exp2(scores - now), axis=0, keepdims=True
        )

    def close(left, pair):
        total[left] = total[left] + (peak[pair] + jnp.log2(mass[pair])) * (
            math.log(2.0) / INV_TEMP
        )

    local.wait()
    set_bias(0, lens_ref[...])
    normalise(0)

    def own(k, carry):
        rows = pl.ds(pl.multiple_of(k * ROWS, ROWS), ROWS)
        tile(units[1, rows], 1, k, 0, 0)
        return carry

    lax.fori_loop(0, chunks, own, 0)
    close(0, 0)

    lens_c.wait()
    block_c.wait()
    set_bias(1, lens[1])
    normalise(1)

    def near(i, carry):
        a, k = i // chunks, lax.rem(i, chunks)
        rows = pl.ds(pl.multiple_of(k * ROWS, ROWS), ROWS)
        slot = answers + lax.rem(a + parity, 2)
        tile(units[slot, rows], slot, k, a, 1 + a)
        return carry

    lax.fori_loop(0, answers * chunks, near, 0)
    for a in range(answers):
        close(a, 1 + a)

    lens_r.wait()
    set_bias(2, lens[2])
    first = 1 + answers

    def far(k, carry):
        piece(k).wait()
        rows = pl.ds(pl.multiple_of(k * ROWS, ROWS), ROWS)
        for b in range(answers):
            fresh[b] = unit_rows(raw[2, b, rows])

        def one(p, carry):
            cross = p < answers * answers
            left = jnp.where(cross, answers + p // answers, p - answers * answers)
            b = jnp.where(cross, lax.rem(p, answers), lax.rem(left + parity, 2))
            tile(fresh[b], 2 * answers + b, k, left, first + p)
            return carry

        lax.fori_loop(0, answers * answers + answers, one, 0)
        return carry

    lax.fori_loop(0, chunks, far, 0)

    back_r = remote(total.at[pl.ds(2 * answers, answers)], back.at[1], chunks + 3, other)
    back_c = remote(total.at[pl.ds(answers, answers)], back.at[0], chunks + 4, partner)
    back_r.start()
    for p in range(answers * answers):
        close(answers + p // answers, first + p)
    back_c.start()
    for a in range(answers):
        close(a, first + answers * answers + a)
    back_c.wait()
    back_r.wait()
    for a in range(answers):
        whole = total[a] + back[0, a] + back[1, a]
        out_ref[a : a + 1] = jnp.where(bias[a] == 0.0, whole / (answers - 1 + 4 * answers), 0.0)


def solution(mesh):
    n = mesh.shape["cand"]

    def shards(embeddings, lengths):
        answers, length, width = embeddings.shape
        chunks = length // ROWS
        pairs = 1 + 2 * answers + answers * answers
        counts = jnp.broadcast_to(lengths[:, None], (answers, 128))
        counts = jnp.pad(counts, ((0, 8 - answers), (0, 0)))
        return pl.pallas_call(
            functools.partial(kernel, n),
            out_shape=jax.ShapeDtypeStruct((answers, length), jnp.float32),
            in_specs=[
                pl.BlockSpec(memory_space=pl.ANY),
                pl.BlockSpec(memory_space=pltpu.VMEM),
            ],
            out_specs=pl.BlockSpec(memory_space=pltpu.VMEM),
            scratch_shapes=[
                pltpu.VMEM((3, answers, length, width), jnp.bfloat16),
                pltpu.VMEM((2 * answers, length, width), jnp.bfloat16),
                pltpu.VMEM((answers, ROWS, width), jnp.bfloat16),
                pltpu.VMEM((3, 8, 128), jnp.int32),
                pltpu.VMEM((3 * answers, 1, length), jnp.float32),
                pltpu.VMEM((pairs, 1, length), jnp.float32),
                pltpu.VMEM((pairs, 1, length), jnp.float32),
                pltpu.VMEM((3 * answers, 1, length), jnp.float32),
                pltpu.VMEM((2, answers, 1, length), jnp.float32),
                pltpu.SemaphoreType.DMA,
                pltpu.SemaphoreType.DMA((chunks + 5,)),
                pltpu.SemaphoreType.DMA((chunks + 5,)),
            ],
            compiler_params=pltpu.CompilerParams(collective_id=0, has_side_effects=True),
            name="consensus",
        )(embeddings, counts)

    return jax.shard_map(
        shards,
        mesh=mesh,
        in_specs=(P(("group", "cand"), None, None), P(("group", "cand"))),
        out_specs=P(("group", "cand"), None),
        check_vma=False,
    )
```

time: 145 us -> 95 us (0.66)
  Pallas kernels: 0 us -> 92.1 us
  waiting for transfers between devices: 86.9 us -> 0 us
  matrix products: 28 us -> 0 us
  other arithmetic: 22.6 us -> 0 us
  starting transfers between devices: 7.58 us -> 0 us
  local copies, waits for them, and re-layouts: 0.01 us -> 2.62 us
    pallas_call x0 -> x1, Pallas kernels: none -> 92.1 us  [shards(): pl.pallas_call(functools.partial(kernel, n), out_shape=jax.ShapeDtypeStru...]
    ppermute x6 -> x0, waiting for transfers between devices: 86.9 us -> none  [from_behind(): lax.ppermute(shard, axis, [(i, (i + by) % count) for i in range(count)])]
    dot_general x5 -> x0, matrix products: 28 us -> none  [soft_terms(): jnp.einsum('te,bse->bts', left, right, preferred_element_type=jnp.float32)]
    reduce_sum x9 -> x0, other arithmetic: 19.2 us -> none  [the longest x3 13.5 us: soft_terms(): jnp.sum(jnp.exp(row_scores - row_peak), axis=2)]
    ppermute x6 -> x0, starting transfers between devices: 7.58 us -> none  [from_behind(): lax.ppermute(shard, axis, [(i, (i + by) % count) for i in range(count)])]
    convert_element_type x2 -> x0, other arithmetic: 2.54 us -> none  [the longest x1 2.46 us: unit_rows(): return (values * scale).astype(jnp.bfloat16)]
  transfers between devices with their start and end apart: 6 -> 0, of which waited for: 4 -> 0; matrix products, arithmetic and copies ran while one was open for 12% -> 0% of each run, Pallas kernels for 0% -> 0%
where the time goes in v1:
time: 95 us; the launch traced here: 94.7 us
  Pallas kernels  92.1 us (97%)
  local copies, waits for them, and re-layouts  2.62 us (3%)
    pallas_call x1, Pallas kernels, shards(): pl.pallas_call(functools.partial(kernel, n), out_shape=jax.ShapeDtypeStru...  92.1 us

profile of v1, /device:TPU:1, one launch (start us, length us, event | category | flops | bytes accessed | tf_op | source)
XLA Modules:
  0.0 94.7 jit_solution(6768034989613694924)
XLA Ops:
  0.0 0.7 pad.6
  0.7 0.7 pad.7.lens_ref
  1.3 92.1 %consensus.1 = f32[2,1024]{1,0:T(2,128)} custom-call(bf16[2,1024,768]{2,1,0:T(8,128)(2,1)} %x_hbm.1, s32[8,128]{1,0:T(8,128)} %pad.7.lens_ref), custom_call_target="tpu_custom_call" | custom-call | tf_op jit(solution)/shard_map/consensus/pallas_call | solution.py:182
  93.4 1.3 %copy.4 = f32[2,1024]{1,0:T(2,128)} copy(f32[2,1024]{1,0:T(2,128)} %consensus.1) | data formatting | bytes 16384

commit v2 on v1

--- a/solution.py
+++ b/solution.py
@@ -1,5 +1,4 @@
 import functools
-import math
 
 import jax
 import jax.numpy as jnp
@@ -12,6 +11,7 @@
 INV_TEMP = 256.0
 LOW = -1e30
 ROWS = 128
+WIDE = 256
 
 
 def unit_rows(raw):
@@ -22,7 +22,7 @@
 
 def kernel(
     n, x_hbm, lens_ref, out_ref,
-    raw, units, fresh, lens, bias, peak, mass, total, back,
+    raw, units, across, fresh, board, lens, bias, peak, mass, total, back,
     local_sem, send_sem, recv_sem,
 ):
     answers, length = x_hbm.shape[0], x_hbm.shape[1]
@@ -75,46 +75,62 @@
         def one(i, carry):
             a, k = i // chunks, lax.rem(i, chunks)
             rows = pl.ds(pl.multiple_of(k * ROWS, ROWS), ROWS)
-            units[slot * answers + a, rows] = unit_rows(raw[slot, a, rows])
+            unit = unit_rows(raw[slot, a, rows])
+            units[slot * answers + a, rows] = unit
+            across[slot * answers + a, :, rows] = unit.T
             return carry
 
         lax.fori_loop(0, answers * chunks, one, 0)
 
-    def tile(query, row_slot, k, left, pair):
+    def score(query, left, place):
+        for j in range(0, length, WIDE):
+            board[pl.ds(place, query.shape[0]), j : j + WIDE] = INV_TEMP * lax.dot_general(
+                query, across[left, :, j : j + WIDE], (((1,), (0,)), ((), ())),
+                preferred_element_type=jnp.float32,
+            ) + bias[left, :, j : j + WIDE]
+
+    def fold(place, row_slot, k, pair):
         cols = pl.ds(pl.multiple_of(k * ROWS, ROWS), ROWS)
         row_bias = jnp.broadcast_to(bias[row_slot, :, cols], (ROWS, ROWS))
         row_bias = jnp.sum(jnp.where(eye, row_bias, 0.0), axis=1, keepdims=True)
-        scores = lax.dot_general(
-            query, units[left], (((1,), (1,)), ((), ())), preferred_element_type=jnp.float32
-        )
-        scores = scores * (INV_TEMP / math.log(2.0)) + bias[left] + row_bias
-        top = jnp.max(scores, axis=1, keepdims=True)
-        row_sum = jnp.sum(jnp.exp2(scores - top), axis=1, keepdims=True)
-        term = (top + jnp.log2(row_sum)) * (math.log(2.0) / INV_TEMP)
+        rows = pl.ds(place, ROWS)
+        tops = None
+        for j in range(0, length, WIDE):
+            scores = board[rows, j : j + WIDE] + row_bias
+            board[rows, j : j + WIDE] = scores
+            before = peak[pair, :, j : j + WIDE]
+            now = jnp.maximum(before, jnp.max(scores, axis=0, keepdims=True))
+            peak[pair, :, j : j + WIDE] = now
+            mass[pair, :, j : j + WIDE] = mass[pair, :, j : j + WIDE] * jnp.exp(
+                before - now
+            ) + jnp.sum(jnp.exp(scores - now), axis=0, keepdims=True)
+            for i in range(0, WIDE, 128):
+                part = scores[:, i : i + 128]
+                tops = part if tops is None else jnp.maximum(tops, part)
+        top = jnp.max(tops, axis=1, keepdims=True)
+        sums = None
+        for j in range(0, length, 128):
+            part = jnp.exp(board[rows, j : j + 128] - top)
+            sums = part if sums is None else sums + part
+        term = (top + jnp.log(jnp.sum(sums, axis=1, keepdims=True))) / INV_TEMP
         term = jnp.sum(jnp.where(eye, jnp.broadcast_to(term, (ROWS, ROWS)), 0.0), axis=0, keepdims=True)
         total[row_slot, :, cols] = total[row_slot, :, cols] + term
-        before = peak[pair]
-        now = jnp.maximum(before, jnp.max(scores, axis=0, keepdims=True))
-        peak[pair] = now
-        mass[pair] = mass[pair] * jnp.exp2(before - now) + jnp.sum(
-            jnp.exp2(scores - now), axis=0, keepdims=True
-        )
 
     def close(left, pair):
-        total[left] = total[left] + (peak[pair] + jnp.log2(mass[pair])) * (
-            math.log(2.0) / INV_TEMP
-        )
+        total[left] = total[left] + (peak[pair] + jnp.log(mass[pair])) / INV_TEMP
 
     local.wait()
     set_bias(0, lens_ref[...])
     normalise(0)
 
     def own(k, carry):
-        rows = pl.ds(pl.multiple_of(k * ROWS, ROWS), ROWS)
-        tile(units[1, rows], 1, k, 0, 0)
+        rows = pl.ds(pl.multiple_of(k * (2 * ROWS), 2 * ROWS), 2 * ROWS)
+        score(units[1, rows], 0, 0)
+        for h in range(2):
+            fold(h * ROWS, 1, 2 * k + h, 0)
         return carry
 
-    lax.fori_loop(0, chunks, own, 0)
+    lax.fori_loop(0, chunks // 2, own, 0)
     close(0, 0)
 
     lens_c.wait()
@@ -122,14 +138,18 @@
     set_bias(1, lens[1])
     normalise(1)
 
-    def near(i, carry):
-        a, k = i // chunks, lax.rem(i, chunks)
-        rows = pl.ds(pl.multiple_of(k * ROWS, ROWS), ROWS)
-        slot = answers + lax.rem(a + parity, 2)
-        tile(units[slot, rows], slot, k, a, 1 + a)
+    def near(k, carry):
+        rows = pl.ds(pl.multiple_of(k * (2 * ROWS), 2 * ROWS), 2 * ROWS)
+        for a in range(answers):
+            slot = answers + lax.rem(a + parity, 2)
+            score(units[slot, rows], a, a * 2 * ROWS)
+        for a in range(answers):
+            slot = answers + lax.rem(a + parity, 2)
+            for h in range(2):
+                fold((2 * a + h) * ROWS, slot, 2 * k + h, 1 + a)
         return carry
 
-    lax.fori_loop(0, answers * chunks, near, 0)
+    lax.fori_loop(0, chunks // 2, near, 0)
     for a in range(answers):
         close(a, 1 + a)
 
@@ -141,16 +161,20 @@
         piece(k).wait()
         rows = pl.ds(pl.multiple_of(k * ROWS, ROWS), ROWS)
         for b in range(answers):
-            fresh[b] = unit_rows(raw[2, b, rows])
-
-        def one(p, carry):
-            cross = p < answers * answers
-            left = jnp.where(cross, answers + p // answers, p - answers * answers)
-            b = jnp.where(cross, lax.rem(p, answers), lax.rem(left + parity, 2))
-            tile(fresh[b], 2 * answers + b, k, left, first + p)
-            return carry
-
-        lax.fori_loop(0, answers * answers + answers, one, 0)
+            fresh[pl.ds(b * ROWS, ROWS)] = unit_rows(raw[2, b, rows])
+        for a in range(answers):
+            score(fresh[...], answers + a, a * answers * ROWS)
+        for a in range(answers):
+            b = lax.rem(a + parity, 2)
+            mine = fresh[pl.ds(pl.multiple_of(b * ROWS, ROWS), ROWS)]
+            score(mine, a, (answers * answers + a) * ROWS)
+        for a in range(answers):
+            for b in range(answers):
+                p = a * answers + b
+                fold(p * ROWS, 2 * answers + b, k, first + p)
+        for a in range(answers):
+            p = answers * answers + a
+            fold(p * ROWS, 2 * answers + lax.rem(a + parity, 2), k, first + p)
         return carry
 
     lax.fori_loop(0, chunks, far, 0)
@@ -190,7 +214,9 @@
             scratch_shapes=[
                 pltpu.VMEM((3, answers, length, width), jnp.bfloat16),
                 pltpu.VMEM((2 * answers, length, width), jnp.bfloat16),
-                pltpu.VMEM((answers, ROWS, width), jnp.bfloat16),
+                pltpu.VMEM((2 * answers, width, length), jnp.bfloat16),
+                pltpu.VMEM((answers * ROWS, width), jnp.bfloat16),
+                pltpu.VMEM((answers * (answers + 1) * ROWS, length), jnp.float32),
                 pltpu.VMEM((3, 8, 128), jnp.int32),
                 pltpu.VMEM((3 * answers, 1, length), jnp.float32),
                 pltpu.VMEM((pairs, 1, length), jnp.float32),

time: 95 us -> 81.5 us (0.86)
  Pallas kernels: 92.1 us -> 78.7 us
    pallas_call x1, Pallas kernels: 92.1 us -> 78.7 us  [shards(): pl.pallas_call(functools.partial(kernel, n), out_shape=jax.ShapeDtypeStru...]
where the time goes in v2:
time: 81.5 us; the launch traced here: 81.3 us
  Pallas kernels  78.7 us (97%)
  local copies, waits for them, and re-layouts  2.62 us (3%)
    pallas_call x1, Pallas kernels, shards(): pl.pallas_call(functools.partial(kernel, n), out_shape=jax.ShapeDtypeStru...  78.7 us

profile of v2, /device:TPU:1, one launch (start us, length us, event | category | flops | bytes accessed | tf_op | source)
XLA Modules:
  0.0 81.3 jit_solution(12325986191970868968)
XLA Ops:
  0.0 0.7 pad.6
  0.7 0.7 pad.7.lens_ref
  1.3 78.7 %consensus.1 = f32[2,1024]{1,0:T(2,128)} custom-call(bf16[2,1024,768]{2,1,0:T(8,128)(2,1)} %x_hbm.1, s32[8,128]{1,0:T(8,128)} %pad.7.lens_ref), custom_call_target="tpu_custom_call" | custom-call | tf_op jit(solution)/shard_map/consensus/pallas_call | solution.py:206
  80.0 1.3 %copy.4 = f32[2,1024]{1,0:T(2,128)} copy(f32[2,1024]{1,0:T(2,128)} %consensus.1) | data formatting | bytes 16384

commit v3 on v2

--- a/solution.py
+++ b/solution.py
@@ -27,10 +27,14 @@
 ):
     answers, length = x_hbm.shape[0], x_hbm.shape[1]
     chunks = length // ROWS
+    pieces = answers * chunks
     me = lax.axis_index("cand")
     parity = lax.rem(me, 2)
     partner = me + 1 - 2 * parity
     other = lax.rem(me + n - 1 + 2 * parity, n)
+
+    for a in range(answers):
+        lens[0, a : a + 1] = jnp.full((1, 128), lens_ref[a], jnp.int32)
 
     barrier = pltpu.get_barrier_semaphore()
     for device in (partner, other):
@@ -45,19 +49,23 @@
             device_id={"cand": device}, device_id_type=MESH,
         )
 
-    def piece(k):
+    def piece(i):
+        b, k = lax.rem(i, answers), i // answers
         rows = pl.ds(pl.multiple_of(k * ROWS, ROWS), ROWS)
-        return remote(x_hbm.at[:, rows], raw.at[2, :, rows], k, other)
-
-    lens_c = remote(lens_ref, lens.at[1], chunks, partner)
-    lens_r = remote(lens_ref, lens.at[2], chunks + 1, other)
-    block_c = remote(x_hbm, raw.at[1], chunks + 2, partner)
+        return remote(x_hbm.at[b, rows], raw.at[2, b, rows], i, other)
+
+    lens_c = remote(lens.at[0], lens.at[1], pieces, partner)
+    lens_r = remote(lens.at[0], lens.at[2], pieces + 1, other)
+    block_c = remote(x_hbm, raw.at[1], pieces + 2, partner)
     lens_r.start()
     lens_c.start()
-    for k in range(chunks):
-        piece(k).start()
-        if k == 0:
-            block_c.start()
+    block_c.start()
+
+    def launch(i, carry):
+        piece(i).start()
+        return carry
+
+    lax.fori_loop(0, pieces, launch, 0)
 
     lane = lax.broadcasted_iota(jnp.int32, (1, length), 1)
     eye = lax.broadcasted_iota(jnp.int32, (ROWS, ROWS), 0) == lax.broadcasted_iota(
@@ -120,7 +128,7 @@
         total[left] = total[left] + (peak[pair] + jnp.log(mass[pair])) / INV_TEMP
 
     local.wait()
-    set_bias(0, lens_ref[...])
+    set_bias(0, lens[0])
     normalise(0)
 
     def own(k, carry):
@@ -157,41 +165,35 @@
     set_bias(2, lens[2])
     first = 1 + answers
 
-    def far(k, carry):
-        piece(k).wait()
+    def far(i, carry):
+        piece(i).wait()
+        k, b = i // answers, lax.rem(i, answers)
         rows = pl.ds(pl.multiple_of(k * ROWS, ROWS), ROWS)
-        for b in range(answers):
-            fresh[pl.ds(b * ROWS, ROWS)] = unit_rows(raw[2, b, rows])
-        for a in range(answers):
-            score(fresh[...], answers + a, a * answers * ROWS)
-        for a in range(answers):
-            b = lax.rem(a + parity, 2)
-            mine = fresh[pl.ds(pl.multiple_of(b * ROWS, ROWS), ROWS)]
-            score(mine, a, (answers * answers + a) * ROWS)
-        for a in range(answers):
-            for b in range(answers):
-                p = a * answers + b
-                fold(p * ROWS, 2 * answers + b, k, first + p)
-        for a in range(answers):
-            p = answers * answers + a
-            fold(p * ROWS, 2 * answers + lax.rem(a + parity, 2), k, first + p)
-        return carry
-
-    lax.fori_loop(0, chunks, far, 0)
-
-    back_r = remote(total.at[pl.ds(2 * answers, answers)], back.at[1], chunks + 3, other)
-    back_c = remote(total.at[pl.ds(answers, answers)], back.at[0], chunks + 4, partner)
-    back_r.start()
+        fresh[...] = unit_rows(raw[2, b, rows])
+        mine = lax.rem(b + parity, answers)
+        for a in range(answers):
+            score(fresh[...], answers + a, a * ROWS)
+        score(fresh[...], mine, answers * ROWS)
+        for a in range(answers):
+            fold(a * ROWS, 2 * answers + b, k, first + a * answers + b)
+        fold(answers * ROWS, 2 * answers + b, k, first + answers * answers + mine)
+        return carry
+
+    lax.fori_loop(0, answers * chunks, far, 0)
+
+    back_r = remote(total.at[pl.ds(2 * answers, answers)], back.at[1], pieces + 3, other)
+    back_c = remote(total.at[pl.ds(answers, answers)], back.at[0], pieces + 4, partner)
     for p in range(answers * answers):
         close(answers + p // answers, first + p)
+    back_r.start()
+    for a in range(answers):
+        close(a, first + answers * answers + a)
     back_c.start()
-    for a in range(answers):
-        close(a, first + answers * answers + a)
     back_c.wait()
     back_r.wait()
     for a in range(answers):
         whole = total[a] + back[0, a] + back[1, a]
-        out_ref[a : a + 1] = jnp.where(bias[a] == 0.0, whole / (answers - 1 + 4 * answers), 0.0)
+        out_ref[a : a + 1] = jnp.where(bias[a] == 0.0, whole, 0.0)
 
 
 def solution(mesh):
@@ -201,35 +203,34 @@
         answers, length, width = embeddings.shape
         chunks = length // ROWS
         pairs = 1 + 2 * answers + answers * answers
-        counts = jnp.broadcast_to(lengths[:, None], (answers, 128))
-        counts = jnp.pad(counts, ((0, 8 - answers), (0, 0)))
-        return pl.pallas_call(
+        sums = pl.pallas_call(
             functools.partial(kernel, n),
             out_shape=jax.ShapeDtypeStruct((answers, length), jnp.float32),
             in_specs=[
                 pl.BlockSpec(memory_space=pl.ANY),
-                pl.BlockSpec(memory_space=pltpu.VMEM),
+                pl.BlockSpec(memory_space=pltpu.SMEM),
             ],
             out_specs=pl.BlockSpec(memory_space=pltpu.VMEM),
             scratch_shapes=[
                 pltpu.VMEM((3, answers, length, width), jnp.bfloat16),
                 pltpu.VMEM((2 * answers, length, width), jnp.bfloat16),
                 pltpu.VMEM((2 * answers, width, length), jnp.bfloat16),
-                pltpu.VMEM((answers * ROWS, width), jnp.bfloat16),
-                pltpu.VMEM((answers * (answers + 1) * ROWS, length), jnp.float32),
-                pltpu.VMEM((3, 8, 128), jnp.int32),
+                pltpu.VMEM((ROWS, width), jnp.bfloat16),
+                pltpu.VMEM((2 * answers * ROWS, length), jnp.float32),
+                pltpu.VMEM((3, answers, 128), jnp.int32),
                 pltpu.VMEM((3 * answers, 1, length), jnp.float32),
                 pltpu.VMEM((pairs, 1, length), jnp.float32),
                 pltpu.VMEM((pairs, 1, length), jnp.float32),
                 pltpu.VMEM((3 * answers, 1, length), jnp.float32),
                 pltpu.VMEM((2, answers, 1, length), jnp.float32),
                 pltpu.SemaphoreType.DMA,
-                pltpu.SemaphoreType.DMA((chunks + 5,)),
-                pltpu.SemaphoreType.DMA((chunks + 5,)),
+                pltpu.SemaphoreType.DMA((answers * chunks + 5,)),
+                pltpu.SemaphoreType.DMA((answers * chunks + 5,)),
             ],
             compiler_params=pltpu.CompilerParams(collective_id=0, has_side_effects=True),
             name="consensus",
-        )(embeddings, counts)
+        )(embeddings, lengths)
+        return sums / (answers - 1 + 4 * answers)
 
     return jax.shard_map(
         shards,

time: 81.5 us -> 79.2 us (0.972)
  local copies, waits for them, and re-layouts: 2.62 us -> 0 us
  other arithmetic: 0 us -> 1.3 us
  Pallas kernels: 78.7 us -> 77.7 us
    pad x2 -> x0, local copies, waits for them, and re-layouts: 1.32 us -> none  [shards(): counts = jnp.pad(counts, ((0, 8 - answers), (0, 0)))]
    div x0 -> x1, other arithmetic: none -> 1.3 us  [shards(): return sums / (answers - 1 + 4 * answers)]
    unnamed x1 -> x0, local copies, waits for them, and re-layouts: 1.3 us -> none
    pallas_call x1, Pallas kernels: 78.7 us -> 77.7 us  [shards(): pl.pallas_call(functools.partial(kernel, n), out_shape=jax.ShapeDtypeStru...]
where the time goes in v3:
time: 79.2 us; the launch traced here: 79 us
  Pallas kernels  77.7 us (98%)
  other arithmetic  1.3 us (2%)
    pallas_call x1, Pallas kernels, shards(): pl.pallas_call(functools.partial(kernel, n), out_shape=jax.ShapeDtypeStru...  77.7 us

profile of v3, /device:TPU:1, one launch (start us, length us, event | category | flops | bytes accessed | tf_op | source)
XLA Modules:
  0.0 79.0 jit_solution(14472730203430326853)
XLA Ops:
  0.0 77.7 %consensus.1 = f32[2,1024]{1,0:T(2,128)} custom-call(bf16[2,1024,768]{2,1,0:T(8,128)(2,1)} %x_hbm.1, s32[2]{0:T(128)} %lens_ref.1), custom_call_target="tpu_custom_call" | custom-call | tf_op jit(solution)/shard_map/consensus/pallas_call | solution.py:206
  77.7 1.3 %broadcast_multiply_fusion = f32[2,1024]{1,0:T(2,128)} fusion(f32[2,1024]{1,0:T(2,128)} %consensus.1), kind=kLoop, calls=%fused_computation | loop fusion | flops 2048 | bytes 16384 | tf_op jit(solution)/shard_map/div | solution.py:233

commit v4 on v3

--- a/solution.py
+++ b/solution.py
@@ -97,10 +97,15 @@
                 preferred_element_type=jnp.float32,
             ) + bias[left, :, j : j + WIDE]
 
-    def fold(place, row_slot, k, pair):
+    def fold(tiles, row_slot, k):
         cols = pl.ds(pl.multiple_of(k * ROWS, ROWS), ROWS)
         row_bias = jnp.broadcast_to(bias[row_slot, :, cols], (ROWS, ROWS))
         row_bias = jnp.sum(jnp.where(eye, row_bias, 0.0), axis=1, keepdims=True)
+        term = sum(soften(place, row_bias, pair) for place, pair in tiles)
+        term = jnp.sum(jnp.where(eye, jnp.broadcast_to(term, (ROWS, ROWS)), 0.0), axis=0, keepdims=True)
+        total[row_slot, :, cols] = total[row_slot, :, cols] + term
+
+    def soften(place, row_bias, pair):
         rows = pl.ds(place, ROWS)
         tops = None
         for j in range(0, length, WIDE):
@@ -120,9 +125,7 @@
         for j in range(0, length, 128):
             part = jnp.exp(board[rows, j : j + 128] - top)
             sums = part if sums is None else sums + part
-        term = (top + jnp.log(jnp.sum(sums, axis=1, keepdims=True))) / INV_TEMP
-        term = jnp.sum(jnp.where(eye, jnp.broadcast_to(term, (ROWS, ROWS)), 0.0), axis=0, keepdims=True)
-        total[row_slot, :, cols] = total[row_slot, :, cols] + term
+        return (top + jnp.log(jnp.sum(sums, axis=1, keepdims=True))) / INV_TEMP
 
     def close(left, pair):
         total[left] = total[left] + (peak[pair] + jnp.log(mass[pair])) / INV_TEMP
@@ -135,7 +138,7 @@
         rows = pl.ds(pl.multiple_of(k * (2 * ROWS), 2 * ROWS), 2 * ROWS)
         score(units[1, rows], 0, 0)
         for h in range(2):
-            fold(h * ROWS, 1, 2 * k + h, 0)
+            fold([(h * ROWS, 0)], 1, 2 * k + h)
         return carry
 
     lax.fori_loop(0, chunks // 2, own, 0)
@@ -154,7 +157,7 @@
         for a in range(answers):
             slot = answers + lax.rem(a + parity, 2)
             for h in range(2):
-                fold((2 * a + h) * ROWS, slot, 2 * k + h, 1 + a)
+                fold([((2 * a + h) * ROWS, 1 + a)], slot, 2 * k + h)
         return carry
 
     lax.fori_loop(0, chunks // 2, near, 0)
@@ -174,9 +177,9 @@
         for a in range(answers):
             score(fresh[...], answers + a, a * ROWS)
         score(fresh[...], mine, answers * ROWS)
-        for a in range(answers):
-            fold(a * ROWS, 2 * answers + b, k, first + a * answers + b)
-        fold(answers * ROWS, 2 * answers + b, k, first + answers * answers + mine)
+        tiles = [(a * ROWS, first + a * answers + b) for a in range(answers)]
+        tiles.append((answers * ROWS, first + answers * answers + mine))
+        fold(tiles, 2 * answers + b, k)
         return carry
 
     lax.fori_loop(0, answers * chunks, far, 0)

time: 79.2 us -> 79.2 us (level)
  no operation moved by 1% of the time
where the time goes in v4:
time: 79.2 us; the launch traced here: 79 us
  Pallas kernels  77.7 us (98%)
  other arithmetic  1.3 us (2%)
    pallas_call x1, Pallas kernels, shards(): pl.pallas_call(functools.partial(kernel, n), out_shape=jax.ShapeDtypeStru...  77.7 us

profile of v4, /device:TPU:1, one launch (start us, length us, event | category | flops | bytes accessed | tf_op | source)
XLA Modules:
  0.0 79.0 jit_solution(3009691939001798421)
XLA Ops:
  0.0 77.7 %consensus.1 = f32[2,1024]{1,0:T(2,128)} custom-call(bf16[2,1024,768]{2,1,0:T(8,128)(2,1)} %x_hbm.1, s32[2]{0:T(128)} %lens_ref.1), custom_call_target="tpu_custom_call" | custom-call | tf_op jit(solution)/shard_map/consensus/pallas_call | solution.py:209
  77.7 1.3 %broadcast_multiply_fusion = f32[2,1024]{1,0:T(2,128)} fusion(f32[2,1024]{1,0:T(2,128)} %consensus.1), kind=kLoop, calls=%fused_computation | loop fusion | flops 2048 | bytes 16384 | tf_op jit(solution)/shard_map/div | solution.py:236
